TPU v7x, 512 devices: a whole 4x8x8 slice. The times are simulated.
512 devices in a mesh: dp: 16 (over z_lo, x), seq: 32 (over z_hi, y, core).
Axes of the slice: x: 4, y: 8, z: 8 (z_hi: 2, z_lo: 4; z = z_hi * 4 + z_lo), core: 2. Of those that a mesh axis runs over, the one named last changes fastest.
Arguments:
- qkv: bfloat16 [3, 16, 2, 2048, 4096], P(None, 'dp', None, 'seq'), may hold values from -4 to 4
- master: float32 [4, 4096], P(None, 'dp'), may hold values from -0.9 to 5.2
- moment_one: float32 [4, 4096], P(None, 'dp'), may hold values from -3 to 3
- moment_two: float32 [4, 4096], P(None, 'dp'), may hold values from 0.25 to 4
- grads: float32 [4, 4096], P(None, 'dp'), may hold values from -8 to 8
Outputs:
- attended: bfloat16 [16, 2, 2048, 4096], P('dp', None, 'seq')
- updated: float32 [4, 4096], P(None, 'dp')
- first_moment: float32 [4, 4096], P(None, 'dp')
- second_moment: float32 [4, 4096], P(None, 'dp')
All inputs are finite; a program needn't handle non-finite values.
Results may differ from a plain program's by a relative error of at most 0.0011.
The roundings to bfloat16 on the way count: a program that leaves them out, or rounds other values in their place, can miss the bound.
Values may be sent and summed in bfloat16 or wider, within the bound.
A program may use at most 64 MiB of HBM per device.

v0:
```python
import jax
import jax.numpy as jnp
from jax import lax
from jax.sharding import PartitionSpec as P

HEADS = 32
HD = 128
OPT_STEP = 10


BETA_ONE = 0.9
BETA_TWO = 0.95
RATE = 0.02
DECAY = 0.1
EPSILON = 1e-08


def from_root(array, axis, root):
    mine = lax.axis_index(axis) == root
    return lax.psum(jnp.where(mine, array, jnp.zeros_like(array)), axis)


def adamw(master, moment_one, moment_two, grads):
    first_moment = BETA_ONE * moment_one + (1.0 - BETA_ONE) * grads
    second_moment = BETA_TWO * moment_two + (1.0 - BETA_TWO) * grads * grads
    first_hat = first_moment / (1.0 - BETA_ONE**OPT_STEP)
    second_hat = second_moment / (1.0 - BETA_TWO**OPT_STEP)
    updated = master - RATE * (first_hat / (jnp.sqrt(second_hat) + EPSILON) + DECAY * master)
    return (updated, first_moment, second_moment)


def normalize(values, gain_row, bias_row):
    row_count = values.shape[0]
    head_count = values.shape[1] // HD
    grouped = values.astype(jnp.float32).reshape(row_count, head_count, HD)
    centre = jnp.mean(grouped, axis=-1, keepdims=True)
    spread = jnp.mean((grouped - centre) ** 2, axis=-1, keepdims=True)
    scaled = (grouped - centre) / jnp.sqrt(spread + 1e-06)
    scaled = scaled * gain_row.reshape(head_count, HD) + bias_row.reshape(head_count, HD)
    return scaled.reshape(row_count, head_count * HD).astype(jnp.bfloat16)


def normalize_block(values, gain_row, bias_row):
    flat = values.reshape(-1, values.shape[-1])
    return normalize(flat, gain_row, bias_row).reshape(values.shape)


def attend(queries, key_rows, value_rows):
    sample_count = queries.shape[0]
    patches = queries.shape[1]
    head_count = queries.shape[2] // HD
    query_heads = queries.reshape(sample_count, patches, head_count, HD)
    key_heads = key_rows.reshape(sample_count, patches, head_count, HD)
    value_heads = value_rows.reshape(sample_count, patches, head_count, HD)
    block_rows = min(512, patches)
    block_count = patches // block_rows
    scale_value = HD ** (-0.5)

    def one_block(position):
        sample_id = position // block_count
        start_row = position % block_count * block_rows
        sample_queries = lax.dynamic_index_in_dim(query_heads, sample_id, 0, keepdims=False)
        sample_keys = lax.dynamic_index_in_dim(key_heads, sample_id, 0, keepdims=False)
        sample_values = lax.dynamic_index_in_dim(value_heads, sample_id, 0, keepdims=False)
        block_queries = lax.dynamic_slice_in_dim(sample_queries, start_row, block_rows, 0)
        scores = (
            jnp.einsum(
                "qhd,khd->hqk", block_queries, sample_keys, preferred_element_type=jnp.float32
            )
            * scale_value
        )
        probs = jax.nn.softmax(scores, axis=-1).astype(jnp.bfloat16)
        block_out = jnp.einsum(
            "hqk,khd->qhd", probs, sample_values, preferred_element_type=jnp.float32
        )
        return block_out.astype(jnp.bfloat16)

    outputs = lax.map(one_block, jnp.arange(sample_count * block_count, dtype=jnp.int32))
    return outputs.reshape(sample_count, patches, head_count * HD)


def shards(qkv, master, moment_one, moment_two, grads):
    updated, first_moment, second_moment = adamw(master, moment_one, moment_two, grads)
    layer_bf = updated.astype(jnp.bfloat16)
    groups = lax.axis_size("seq")
    width = HEADS // groups * HD
    shard_cols = layer_bf.shape[1]
    first_col = lax.axis_index("seq") * width
    owner_index = first_col // shard_cols
    own_layer = from_root(layer_bf, "dp", owner_index).astype(jnp.float32)
    own_part = lax.dynamic_slice_in_dim(own_layer, first_col % shard_cols, width, 1)
    arrived = lax.all_to_all(qkv, "seq", split_axis=4, concat_axis=3, tiled=True)
    queries = normalize_block(arrived[0, 0], own_part[0], own_part[1])
    key_rows = normalize_block(arrived[1, 0], own_part[2], own_part[3])
    head_out = attend(queries, key_rows, arrived[2, 0])[None]
    attended = lax.all_to_all(head_out, "seq", split_axis=2, concat_axis=3, tiled=True)
    return (attended, updated, first_moment, second_moment)


def solution(mesh):
    placed = (
        P(None, "dp", None, "seq", None),
        P(None, "dp"),
        P(None, "dp"),
        P(None, "dp"),
        P(None, "dp"),
    )
    return jax.shard_map(
        shards,
        mesh=mesh,
        in_specs=placed,
        out_specs=(P("dp", None, "seq", None), P(None, "dp"), P(None, "dp"), P(None, "dp")),
        check_vma=False,
    )
```

profile of v0, /device:TPU:8, one launch (start us, length us, event | category | flops | bytes accessed | tf_op | source)
XLA Modules:
  0.0 299.9 jit_solution(16525760995206062326)
XLA Ops:
  0.6 11.8 %copy.78 = bf16[3,1,2,64,4096]{3,0,2,1,4:T(4,128)(2,1)} copy(bf16[3,1,2,64,4096]{4,3,2,1,0:T(8,128)(2,1)} %param.7) | data formatting | bytes 6291456 | tf_op args[0]
  12.4 13.3 %reshape.365 = bf16[32,2,24576]{2,1,0:T(2,128)(2,1)} reshape(bf16[4096,1,2,3,64]{4,3,2,1,0:T(4,128)(2,1)} %bitcast.72) | data formatting | bytes 6291456
  25.7 16.3 %all-to-all-start = ((bf16[32,2,24576]{2,1,0:T(2,128)(2,1)}), bf16[32,2,24576]{2,1,0:T(2,128)(2,1)S(1)}, u32[]{:S(2)}, u32[]{:S(2)}) async-start(bf16[32,2,24576]{2,1,0:T(2,128)(2,1)} %reshape.365), calls=%async_computation | async-start | bytes 6291456 | tf_op jit(solution)/shard_map/all_to_all | solution.py:92
  42.1 0.6 convert_select_fusion
  42.7 92.8 %psum.7 = bf16[4,256]{1,0:T(4,128)(2,1)S(1)} all-reduce(bf16[4,256]{1,0:T(4,128)(2,1)S(1)} %get-tuple-element.168), channel_id=1, replica_groups=mesh['dp'=16,'seq'=32] {'dp'}, use_global_device_ids=true, to_apply=%region_2.3 | all-reduce | flops 1024 | bytes 4096 | tf_op jit(solution)/shard_map/psum | solution.py:20
  135.6 9.3 %reshape.366 = bf16[4096,1,2,3,64]{4,3,2,1,0:T(4,128)(2,1)} reshape(bf16[32,2,24576]{2,1,0:T(2,128)(2,1)S(1)} %all-to-all-done) | data formatting | bytes 6291456
  144.8 8.1 %copy.94 = bf16[3,1,2,64,32,128]{5,4,3,2,0,1:T(8,128)(2,1)S(1)} copy(bf16[3,1,2,64,32,128]{3,0,2,5,4,1:T(4,128)(2,1)} %bitcast.71) | data formatting | bytes 6291456 | tf_op jit(solution)/shard_map/all_to_all | solution.py:92
  153.0 2.6 slice_convert_fusion
  155.6 1.1 fusion.21
  157.3 2.8 copy.84
  160.1 1.4 fusion.15
  161.6 2.8 copy.81
  164.4 1.3 copy-done
  165.7 1.4 fusion.17
  167.2 1.4 copy.80
  168.6 0.6 copy-done.1
  169.2 3.8 %fusion.18 = (bf16[2,2048,1,128]{3,1,2,0:T(8,128)(2,1)}, bf16[2,2048,1,128]{3,1,2,0:T(8,128)(2,1)S(1)}) fusion(f32[128]{0:T(128)S(1)} %get-tuple-element.178, f32[128]{0:T(128)S(1)} %get-tuple-element.179, f32[2,2048]{1,0:T(2,128)S(1)} %sqrt.26, f32[2,2048,1,128]{3,1,0,2:T(8,128)S(1)} %bitcast.76, f32[2,2048]{1,0:T(2,128)S(1)} %div.100, ...), kind=kLoop, calls=%fused_computation.29 | loop fusion | flops 5242880 | bytes 6359040 | tf_op jit(solution)/shard_map/while | solution.py:78
  173.0 67.5 %while.13 = (s32[]{:T(128)}, bf16[8,512,1,128]{3,1,0,2:T(8,128)(2,1)}, s32[8]{0:T(128)S(1)}, bf16[2,2048,1,128]{3,1,2,0:T(8,128)(2,1)}, bf16[2,2048,1,128]{3,1,2...) while((s32[]{:T(128)}, ...), condition=%wide.region_8.9_spmd, body=%wide.region_5.8_spmd.sunk | while | flops 546372608 | bytes 18623472 | solution.py:78
  173.0 0.7 dynamic_slice.56
  176.4 1.7 multiply_reduce_fusion.2
  178.2 0.8 fusion.28
  179.4 1.2 fusion.29
  180.7 0.7 constant_dynamic-update-slice_fusion.2
  181.4 0.7 dynamic_slice.56
  184.9 1.7 multiply_reduce_fusion.2
  186.6 0.8 fusion.28
  187.8 1.2 fusion.29
  189.2 0.7 constant_dynamic-update-slice_fusion.2
  189.9 0.7 dynamic_slice.56
  193.3 1.7 multiply_reduce_fusion.2
  195.0 0.8 fusion.28
  196.3 1.2 fusion.29
  197.6 0.7 constant_dynamic-update-slice_fusion.2
  198.3 0.7 dynamic_slice.56
  201.8 1.7 multiply_reduce_fusion.2
  203.5 0.8 fusion.28
  204.3 0.4 copy-done.3
  204.7 1.2 fusion.29
  206.1 0.7 constant_dynamic-update-slice_fusion.2
  206.7 0.7 dynamic_slice.56
  210.2 1.7 multiply_reduce_fusion.2
  211.9 0.8 fusion.28
  212.7 0.4 copy-done.3
  213.1 1.2 fusion.29
  214.5 0.7 constant_dynamic-update-slice_fusion.2
  215.2 0.7 dynamic_slice.56
  218.6 1.7 multiply_reduce_fusion.2
  220.4 0.8 fusion.28
  221.2 0.4 copy-done.3
  221.6 1.2 fusion.29
  222.9 0.7 constant_dynamic-update-slice_fusion.2
  223.6 0.7 dynamic_slice.56
  227.1 1.7 multiply_reduce_fusion.2
  228.8 0.8 fusion.28
  230.0 1.2 fusion.29
  231.4 0.7 constant_dynamic-update-slice_fusion.2
  232.0 0.7 dynamic_slice.56
  235.5 1.7 multiply_reduce_fusion.2
  237.2 0.8 fusion.28
  238.5 1.2 fusion.29
  239.8 0.7 constant_dynamic-update-slice_fusion.2
  240.5 2.8 copy.91
  243.3 55.2 %all_to_all.33 = bf16[1,2,2048,128]{3,1,0,2:T(2,128)(2,1)S(1)} all-to-all(bf16[1,2,2048,128]{3,1,0,2:T(2,128)(2,1)S(1)} %copy.91), channel_id=1, replica_groups=mesh['dp'=16,'seq'=32] {'seq'}, dimensions={2} | all-to-all | bytes 2097152 | tf_op jit(solution)/shard_map/all_to_all | solution.py:96
  298.6 1.2 copy.99
  (51 shorter events, 3.7 us)
Async XLA Ops:
  25.7 16.4 %copy-start.4 = (f32[4,256]{1,0:T(4,128)S(1)}, f32[4,256]{1,0:T(4,128)}, u32[]{:S(2)}) copy-start(f32[4,256]{1,0:T(4,128)} %param.8) | copy-start | bytes 12292
  25.7 16.4 %copy-start.5 = (f32[4,256]{1,0:T(4,128)S(1)}, f32[4,256]{1,0:T(4,128)}, u32[]{:S(2)}) copy-start(f32[4,256]{1,0:T(4,128)} %param.11) | copy-start | bytes 12292
  25.7 16.4 %copy-start.6 = (f32[4,256]{1,0:T(4,128)S(1)}, f32[4,256]{1,0:T(4,128)}, u32[]{:S(2)}) copy-start(f32[4,256]{1,0:T(4,128)} %param.9) | copy-start | bytes 12292
  25.7 16.4 %copy-start.7 = (f32[4,256]{1,0:T(4,128)S(1)}, f32[4,256]{1,0:T(4,128)}, u32[]{:S(2)}) copy-start(f32[4,256]{1,0:T(4,128)} %param.10) | copy-start | bytes 12292
  25.7 109.8 %all-to-all-start = ((bf16[32,2,24576]{2,1,0:T(2,128)(2,1)}), bf16[32,2,24576]{2,1,0:T(2,128)(2,1)S(1)}, u32[]{:S(2)}, u32[]{:S(2)}) async-start(bf16[32,2,24576]{2,1,0:T(2,128)(2,1)} %reshape.365), calls=%async_computation | async-start | bytes 6291456 | tf_op jit(solution)/shard_map/all_to_all | solution.py:92
  164.4 1.4 copy-start
  165.7 1.5 copy-start.2
  167.2 2.0 copy-start.1
  178.2 1.2 copy-start.3
  186.6 1.2 copy-start.3
  195.0 1.2 copy-start.3
  203.5 1.2 copy-start.3
  211.9 1.2 copy-start.3
  220.4 1.2 copy-start.3
  228.8 1.2 copy-start.3
  237.2 1.2 copy-start.3
where the time goes:
time: 302 us; the launch traced here: 300 us
  blocking collectives  148 us (49%)
  local copies, waits for them, and re-layouts  71 us (24%)
  matrix products  23.5 us (8%)
  loops' own time  22.6 us (7%)
  other arithmetic  17.7 us (6%)
  starting transfers between devices  16.3 us (5%)
    psum x1, blocking collectives, from_root(): return lax.psum(jnp.where(mine, array, jnp.zeros_like(array)), axis)  92.8 us
    all_to_all x1, blocking collectives, shards(): lax.all_to_all(head_out, 'seq', split_axis=2, concat_axis=3, tiled=True)  55.2 us
    unnamed x17, local copies, waits for them, and re-layouts  36.3 us
    another operation x1, loops' own time, attend(): lax.map(one_block, jnp.arange(sample_count * block_count, dtype=jnp.int32))  22.6 us
    all_to_all x1, starting transfers between devices, shards(): lax.all_to_all(qkv, 'seq', split_axis=4, concat_axis=3, tiled=True)  16.3 us
    dot_general x8, matrix products, one_block(): jnp.einsum('qhd,khd->hqk', block_queries, sample_keys, preferred_element_...  13.7 us
    dot_general x8, matrix products, one_block(): jnp.einsum('hqk,khd->qhd', probs, sample_values, preferred_element_type=j...  9.8 us
    all_to_all x1, local copies, waits for them, and re-layouts, shards(): lax.all_to_all(qkv, 'seq', split_axis=4, concat_axis=3, tiled=True)  8.14 us
  transfers between devices with their start and end apart: 1, of which 0 were waited for; matrix products, arithmetic and copies ran while one was open for 0% of the time, Pallas kernels for 0%

commit v1 on v0

v1 whole, which is shorter than its diff:
```python
import functools

import jax
import jax.numpy as jnp
from jax import lax
from jax.experimental import pallas as pl
from jax.experimental.pallas import tpu as pltpu
from jax.sharding import PartitionSpec as P

HEADS = 32
HD = 128
OPT_STEP = 10

BETA_ONE = 0.9
BETA_TWO = 0.95
RATE = 0.02
DECAY = 0.1
EPSILON = 1e-08

BLOCK = 256
SCORE_SCALE = HD**-0.5 * 1.4426950408889634
MESH = pl.DeviceIdType.MESH


def adamw(master, moment_one, moment_two, grads):
    first_moment = BETA_ONE * moment_one + (1.0 - BETA_ONE) * grads
    second_moment = BETA_TWO * moment_two + (1.0 - BETA_TWO) * grads * grads
    first_hat = first_moment / (1.0 - BETA_ONE**OPT_STEP)
    second_hat = second_moment / (1.0 - BETA_TWO**OPT_STEP)
    updated = master - RATE * (first_hat / (jnp.sqrt(second_hat) + EPSILON) + DECAY * master)
    return (updated, first_moment, second_moment)


def normalize(values, gain, bias):
    values = values.astype(jnp.float32)
    centred = values - jnp.mean(values, axis=-1, keepdims=True)
    spread = jnp.mean(centred * centred, axis=-1, keepdims=True)
    return (centred / jnp.sqrt(spread + 1e-06) * gain + bias).astype(jnp.bfloat16)


def attend(queries, keys, values):
    scores = lax.dot_general(
        queries, keys, (((1,), (1,)), ((), ())), preferred_element_type=jnp.float32
    )
    top = jnp.max(scores, axis=-1, keepdims=True)
    weights = jnp.exp2((scores - top) * SCORE_SCALE)
    total = jnp.sum(weights, axis=-1, keepdims=True)
    probs = (weights * (1.0 / total)).astype(jnp.bfloat16)
    out = jnp.dot(probs, values, preferred_element_type=jnp.float32)
    return out.astype(jnp.bfloat16)


def peer(step, me):
    turn = step // 4
    hops = (12 + (turn + 1) // 2 * (1 - 2 * (turn % 2))) % 8
    half = (me // 16 + 1 - (step // 2) % 2) % 2
    row = (me // 2 % 8 + hops) % 8
    core = (me + 1 - step % 2) % 2
    return half * 16 + row * 2 + core


def kernel(groups, replicas, qkv, layer, out, got, keys, queries, done, gains, in_sem, in_sent, out_sem, out_sent, gain_sem, gain_sent):
    samples, rows = qkv.shape[2], qkv.shape[3]
    patches = rows * groups
    me = lax.axis_index("seq")
    replica = lax.axis_index("dp")
    owner = me * HD // layer.shape[1]

    barrier = pltpu.get_barrier_semaphore()

    def greet_seq(step, carry):
        pl.semaphore_signal(barrier, 1, device_id=(replica, peer(step, me)), device_id_type=MESH)
        return carry

    def greet_dp(step, carry):
        pl.semaphore_signal(
            barrier, 1, device_id=((replica + step) % replicas, me), device_id_type=MESH
        )
        return carry

    lax.fori_loop(0, groups - 1, greet_seq, 0)
    lax.fori_loop(1, replicas, greet_dp, 0)
    pl.semaphore_wait(barrier, groups - 1 + replicas - 1)

    own_layer = layer.at[:, pl.ds(pl.multiple_of(me * HD % layer.shape[1], HD), HD)]

    @pl.when(replica == owner)
    def _():
        def give(step, carry):
            pltpu.make_async_remote_copy(
                own_layer,
                gains,
                gain_sent,
                gain_sem,
                device_id=((replica + step) % replicas, me),
                device_id_type=MESH,
            ).start()
            return carry

        lax.fori_loop(1, replicas, give, 0)
        pltpu.make_async_copy(own_layer, gains, gain_sem).start()

    mine = pl.ds(pl.multiple_of(me * rows, rows), rows)

    def slice_of(first, count, sample, device):
        columns = pl.ds(pl.multiple_of(device * HD, HD), HD)
        return qkv.at[pl.ds(first, count), 0, sample, :, columns]

    for sample in range(samples):
        for part, (first, count) in enumerate(((1, 2), (0, 1))):
            target = got.at[sample, pl.ds(first, count), mine, :]

            def send(step, carry):
                device = peer(step, me)
                pltpu.make_async_remote_copy(
                    slice_of(first, count, sample, device),
                    target,
                    in_sent.at[sample, part],
                    in_sem.at[sample, part],
                    device_id=(replica, device),
                    device_id_type=MESH,
                ).start()
                return carry

            lax.fori_loop(0, groups - 1, send, 0)
            pltpu.make_async_copy(
                slice_of(first, count, sample, me), target, in_sem.at[sample, part]
            ).start()

    pltpu.make_async_copy(gains, gains, gain_sem).wait()
    table = gains[...].astype(jnp.float32)

    out_columns = pl.ds(pl.multiple_of(me * HD, HD), HD)
    sharers = BLOCK // rows
    blocks = patches // BLOCK
    for sample in range(samples):
        for part, (first, count) in enumerate(((1, 2), (0, 1))):
            whole = got.at[sample, pl.ds(first, count)]
            pltpu.make_async_copy(whole, whole, in_sem.at[sample, part]).wait()
            source = got.at[sample, first]
            target = keys if part == 0 else queries
            gain, bias = (table[2:3], table[3:4]) if part == 0 else (table[0:1], table[1:2])

            def norm_rows(step, carry):
                at = pl.ds(pl.multiple_of(step * BLOCK, BLOCK), BLOCK)
                target[at, :] = normalize(source[at, :], gain, bias)
                return carry

            lax.fori_loop(0, blocks, norm_rows, 0)

        def one_block(step, carry):
            block = (me // sharers + step) % blocks
            at = pl.ds(pl.multiple_of(block * BLOCK, BLOCK), BLOCK)
            done[sample, at, :] = attend(queries[at, :], keys[...], got[sample, 2])
            for share in range(sharers):
                device = block * sharers + share
                source = done.at[sample, pl.ds(pl.multiple_of(device * rows, rows), rows), :]
                target = out.at[0, sample, :, out_columns]

                @pl.when(device != me)
                def _():
                    pltpu.make_async_remote_copy(
                        source,
                        target,
                        out_sent,
                        out_sem,
                        device_id=(replica, device),
                        device_id_type=MESH,
                    ).start()

                @pl.when(device == me)
                def _():
                    pltpu.make_async_copy(source, target, out_sem).start()

            return carry

        lax.fori_loop(0, blocks, one_block, 0)

    others = rows * (groups - 1)
    for sample in range(samples):
        for part, (first, count) in enumerate(((1, 2), (0, 1))):
            sent = got.at[sample, pl.ds(first, count), pl.ds(0, others)]
            pltpu.make_async_copy(sent, sent, in_sent.at[sample, part]).wait()
    sent = done.at[:, pl.ds(0, others)]
    pltpu.make_async_copy(sent, sent, out_sent).wait()
    pltpu.make_async_copy(out, out, out_sem).wait()

    @pl.when(replica == owner)
    def _():
        def gave(step, carry):
            pltpu.make_async_copy(gains, gains, gain_sent).wait()
            return carry

        lax.fori_loop(1, replicas, gave, 0)


def shards(qkv, master, moment_one, moment_two, grads):
    updated, first_moment, second_moment = adamw(master, moment_one, moment_two, grads)
    layer = updated.astype(jnp.bfloat16)
    groups = lax.axis_size("seq")
    replicas = lax.axis_size("dp")
    _, _, samples, rows, width = qkv.shape
    patches = rows * groups
    attended = pl.pallas_call(
        functools.partial(kernel, groups, replicas),
        out_shape=jax.ShapeDtypeStruct((1, samples, rows, width), jnp.bfloat16),
        in_specs=[pl.BlockSpec(memory_space=pl.ANY), pl.BlockSpec(memory_space=pltpu.VMEM)],
        out_specs=pl.BlockSpec(memory_space=pl.ANY),
        scratch_shapes=[
            pltpu.VMEM((samples, 3, patches, HD), jnp.bfloat16),
            pltpu.VMEM((patches, HD), jnp.bfloat16),
            pltpu.VMEM((patches, HD), jnp.bfloat16),
            pltpu.VMEM((samples, patches, HD), jnp.bfloat16),
            pltpu.VMEM((4, HD), jnp.bfloat16),
            pltpu.SemaphoreType.DMA((samples, 2)),
            pltpu.SemaphoreType.DMA((samples, 2)),
            pltpu.SemaphoreType.DMA,
            pltpu.SemaphoreType.DMA,
            pltpu.SemaphoreType.DMA,
            pltpu.SemaphoreType.DMA,
        ],
        compiler_params=pltpu.CompilerParams(
            collective_id=0, has_side_effects=True, vmem_limit_bytes=48 * 1024 * 1024
        ),
    )(qkv, layer)
    return (attended, updated, first_moment, second_moment)


def solution(mesh):
    placed = (
        P(None, "dp", None, "seq", None),
        P(None, "dp"),
        P(None, "dp"),
        P(None, "dp"),
        P(None, "dp"),
    )
    return jax.shard_map(
        shards,
        mesh=mesh,
        in_specs=placed,
        out_specs=(P("dp", None, "seq", None), P(None, "dp"), P(None, "dp"), P(None, "dp")),
        check_vma=False,
    )
```

time: 302 us -> 135 us (0.45)
  the two profiles are of different devices: /device:TPU:8 before, /device:TPU:59 now
where the time goes in v1:
time: 135 us; the launch traced here: 134 us
  Pallas kernels  129 us (96%)
  local copies, waits for them, and re-layouts  2.86 us (2%)
  other arithmetic  1.36 us (1%)
    pallas_call x1, Pallas kernels, shards(): pl.pallas_call(functools.partial(kernel, groups, replicas), out_shape=jax...  129 us
    unnamed x3, local copies, waits for them, and re-layouts  2.86 us

profile of v1, /device:TPU:59, one launch (start us, length us, event | category | flops | bytes accessed | tf_op | source)
XLA Modules:
  0.0 134.3 jit_solution(17090593828098317338)
XLA Ops:
  0.6 1.4 %fusion.1 = (bf16[4,256]{1,0:T(4,128)(2,1)S(1)}, f32[4,256]{1,0:T(4,128)}, f32[4,256]{1,0:T(4,128)}, f32[4,256]{1,0:T(4,128)}) fusion(f32[4,256]{1,0:T(4,128)} %param.6, f32[4,256]{1,0:T(4,128)} %param.9, f32[4,256]{1,0:T(4,128)} %param.7, f32[4,256]{1,0:T(4,128)} %param.8), kind=kLoop, calls=%fused_computation.4 | loop fusion | flops 16384 | bytes 30720 | tf_op jit(solution)/shard_map/convert_element_type | solution.py:199
  2.0 0.0 copy-start
  2.0 1.9 %copy-done = bf16[3,1,2,64,4096]{4,3,2,1,0:T(8,128)(2,1)S(1)} copy-done((bf16[3,1,2,64,4096]{4,3,2,1,0:T(8,128)(2,1)S(1)}, bf16[3,1,2,64,4096]{4,3,2,1,0:T(8,128)(2,1)}, u32[]{:S(2)}) %copy-start) | copy-done | bytes 3145752
  3.9 129.5 %shard_map.84 = bf16[1,2,64,4096]{3,2,1,0:T(8,128)(2,1)S(1)} custom-call(bf16[3,1,2,64,4096]{4,3,2,1,0:T(8,128)(2,1)S(1)} %copy-done, bf16[4,256]{1,0:T(4,128)(2,1)S(1)} %get-tuple-element.4.layer), custom_call_target="tpu_custom_call" | custom-call | tf_op jit(solution)/shard_map/pallas_call | solution.py:204
  133.4 1.0 copy.10
Async XLA Ops:
  2.0 1.9 %copy-start = (bf16[3,1,2,64,4096]{4,3,2,1,0:T(8,128)(2,1)S(1)}, bf16[3,1,2,64,4096]{4,3,2,1,0:T(8,128)(2,1)}, u32[]{:S(2)}) copy-start(bf16[3,1,2,64,4096]{4,3,2,1,0:T(8,128)(2,1)} %qkv.1) | copy-start | bytes 9437188

commit v2 on v1

v2 whole, which is shorter than its diff:
```python
import functools

import jax
import jax.numpy as jnp
from jax import lax
from jax.experimental import pallas as pl
from jax.experimental.pallas import tpu as pltpu
from jax.sharding import PartitionSpec as P

HEADS = 32
HD = 128
OPT_STEP = 10

BETA_ONE = 0.9
BETA_TWO = 0.95
RATE = 0.02
DECAY = 0.1
EPSILON = 1e-08

BLOCK = 256
SCORE_SCALE = HD**-0.5 * 1.4426950408889634
MESH = pl.DeviceIdType.MESH


def adamw(master, moment_one, moment_two, grads):
    first_moment = BETA_ONE * moment_one + (1.0 - BETA_ONE) * grads
    second_moment = BETA_TWO * moment_two + (1.0 - BETA_TWO) * grads * grads
    first_hat = first_moment / (1.0 - BETA_ONE**OPT_STEP)
    second_hat = second_moment / (1.0 - BETA_TWO**OPT_STEP)
    updated = master - RATE * (first_hat / (jnp.sqrt(second_hat) + EPSILON) + DECAY * master)
    return (updated, first_moment, second_moment)


def normalize(values, gain, bias):
    values = values.astype(jnp.float32)
    centred = values - jnp.mean(values, axis=-1, keepdims=True)
    spread = jnp.mean(centred * centred, axis=-1, keepdims=True)
    return (centred / jnp.sqrt(spread + 1e-06) * gain + bias).astype(jnp.bfloat16)


def attend(queries, keys, values):
    scores = lax.dot_general(
        queries, keys, (((1,), (1,)), ((), ())), preferred_element_type=jnp.float32
    )
    top = jnp.max(scores, axis=-1, keepdims=True)
    weights = jnp.exp2((scores - top) * SCORE_SCALE)
    total = jnp.sum(weights, axis=-1, keepdims=True)
    probs = (weights * (1.0 / total)).astype(jnp.bfloat16)
    out = jnp.dot(probs, values, preferred_element_type=jnp.float32)
    return out.astype(jnp.bfloat16)


def loop(count, body):
    def step(index, carry):
        body(index)
        return carry

    lax.fori_loop(0, count, step, 0)


def kernel(groups, replicas, qkv, layer, out, got, by_row, by_half, keys, done, relay, gains,
           got_sem, late_sem, row_sem, half_sem, relay_sem, out_sem, gain_sem,
           near_sent, row_sent, half_sent, out_sent, relay_sent, gain_sent):
    samples, rows = qkv.shape[2], qkv.shape[3]
    half_size = groups // 2
    chips = half_size // 2
    half_rows = rows * half_size
    me = lax.axis_index("seq")
    replica = lax.axis_index("dp")
    half, place = me // half_size, me % half_size
    chip, core = place // 2, place % 2
    opposite = (me + half_size) % groups
    owner = me * HD // layer.shape[1]

    def hops(turn):
        return (chips + chips // 2 + (turn + 1) // 2 * (1 - 2 * (turn % 2))) % chips

    def peer(step):
        return (chip + hops(step // 2)) % chips * 2 + (core + 1 - step % 2) % 2

    def at_rows(device):
        return pl.ds(pl.multiple_of(device * rows, rows), rows)

    def columns(device, count=1):
        return pl.ds(pl.multiple_of(device * HD, HD), count * HD)

    def push(source, target, sent, arrived, device):
        pltpu.make_async_remote_copy(
            source, target, sent, arrived, device_id=(replica, device), device_id_type=MESH
        ).start()

    def keep(source, target, arrived):
        pltpu.make_async_copy(source, target, arrived).start()

    def wait(ref, semaphore):
        pltpu.make_async_copy(ref, ref, semaphore).wait()

    Q, K, V = 0, 1, 2
    pair = 2 * rows
    turns = chips // 2

    def spots(turn):
        distance = turns - turn
        return (chip + distance) % chips, (chip + chips - distance % turns) % chips

    def chip_rows(which, seat):
        return pl.ds(pl.multiple_of(which * half_rows + seat * pair, pair), pair)

    barrier = pltpu.get_barrier_semaphore()

    def greet_row(step, carry):
        device = half * half_size + peer(step)
        pl.semaphore_signal(barrier, 1, device_id=(replica, device), device_id_type=MESH)
        return carry

    def greet_dp(step, carry):
        other = (replica + step) % replicas
        pl.semaphore_signal(barrier, 1, device_id=(other, me), device_id_type=MESH)
        return carry

    lax.fori_loop(0, half_size - 1, greet_row, 0)
    pl.semaphore_signal(barrier, 1, device_id=(replica, opposite), device_id_type=MESH)
    lax.fori_loop(1, replicas, greet_dp, 0)
    pl.semaphore_wait(barrier, half_size - 1 + 1 + replicas - 1)

    own_layer = layer.at[:, pl.ds(pl.multiple_of(me * HD % layer.shape[1], HD), HD)]

    @pl.when(replica == owner)
    def _():
        def give(step, carry):
            pltpu.make_async_remote_copy(
                own_layer,
                gains,
                gain_sent,
                gain_sem,
                device_id=((replica + step) % replicas, me),
                device_id_type=MESH,
            ).start()
            return carry

        lax.fori_loop(1, replicas, give, 0)
        keep(own_layer, gains, gain_sem)

    def near(sample, part):
        target = got.at[sample, part, at_rows(me), :]
        arrived = got_sem.at[sample, part]

        def send(step, carry):
            device = half * half_size + peer(step)
            source = qkv.at[part, 0, sample, :, columns(device)]
            push(source, target, near_sent.at[sample, part], arrived, device)
            return carry

        lax.fori_loop(0, half_size - 1, send, 0)
        keep(qkv.at[part, 0, sample, :, columns(me)], target, arrived)

    def row_first(sample, part, slot):
        target = by_row.at[slot, at_rows(place), :]

        def send(step, carry):
            seat = peer(step)
            source = qkv.at[part, 0, sample, :, columns((1 - half) * half_size + seat)]
            push(source, target, row_sent.at[slot], row_sem.at[slot], half * half_size + seat)
            return carry

        lax.fori_loop(0, half_size - 1, send, 0)
        source = qkv.at[part, 0, sample, :, columns(opposite)]
        keep(source, target, row_sem.at[slot])

    def row_then_half(sample, part, slot):
        wait(by_row.at[slot], row_sem.at[slot])
        at = pl.ds(pl.multiple_of(half * half_rows, half_rows), half_rows)
        push(
            by_row.at[slot], got.at[sample, part, at, :], half_sent.at[slot],
            got_sem.at[sample, part], opposite,
        )

    def row_then_half_by_turn(sample, part, slot):
        wait(by_row.at[slot], row_sem.at[slot])

        def send(turn):
            for seat in spots(turn):
                source = by_row.at[slot, pl.ds(pl.multiple_of(seat * pair, pair), pair), :]
                target = got.at[sample, part, chip_rows(half, seat), :]
                push(source, target, half_sent.at[slot], late_sem.at[turn], opposite)

        loop(turns, send)

    def half_first(sample, part, slot):
        source = qkv.at[part, 0, sample, :, columns((1 - half) * half_size, half_size)]
        push(source, by_half.at[slot], half_sent.at[3 + slot], half_sem.at[slot], opposite)

    def half_then_row(sample, part, slot):
        wait(by_half.at[slot], half_sem.at[slot])
        target = got.at[sample, part, at_rows(opposite), :]
        arrived = got_sem.at[sample, part]

        def send(step, carry):
            seat = peer(step)
            source = by_half.at[slot, :, columns(seat)]
            push(source, target, row_sent.at[3 + slot], arrived, half * half_size + seat)
            return carry

        lax.fori_loop(0, half_size - 1, send, 0)
        keep(by_half.at[slot, :, columns(place)], target, arrived)

    def norm_keys(sample):
        wait(got.at[sample, K], got_sem.at[sample, K])

        def norm_rows(step):
            at = pl.ds(pl.multiple_of(step * BLOCK, BLOCK), BLOCK)
            keys[sample, at, :] = normalize(got[sample, K, at, :], table[2:3], table[3:4])

        loop(keys.shape[1] // BLOCK, norm_rows)

    def attend_turn(sample, turn, which):
        ats = [chip_rows(which, seat) for seat in spots(turn)]
        block = jnp.concatenate([got[sample, Q, at, :] for at in ats], axis=0)
        queries = normalize(block, table[0:1], table[1:2])
        return attend(queries, keys[sample], got[sample, V])

    def far_turn(sample, turn):
        done[sample, 0, turn] = attend_turn(sample, turn, 1 - half)

    def send_far(sample, turn):
        push(
            done.at[sample, 0, turn], relay.at[sample, turn], out_sent.at[0],
            relay_sem.at[sample, turn], opposite,
        )

    def hand_out(source, head, sample, turn, sent):
        target = out.at[0, sample, :, columns(head)]
        for side, seat in enumerate(spots(turn)):
            for unit in range(2):
                piece = source.at[pl.ds(side * pair + unit * rows, rows), :]
                device = half * half_size + seat * 2 + unit

                @pl.when(device != me)
                def _():
                    push(piece, target, sent, out_sem, device)

                @pl.when(device == me)
                def _():
                    keep(piece, target, out_sem)

    def near_turn(sample, turn):
        done[sample, 1, turn] = attend_turn(sample, turn, half)
        hand_out(done.at[sample, 1, turn], me, sample, turn, out_sent.at[1])

    def relay_turn(sample, turn):
        wait(relay.at[sample, turn], relay_sem.at[sample, turn])
        hand_out(relay.at[sample, turn], opposite, sample, turn, relay_sent)

    half_first(0, K, 0)
    row_first(1, K, 0)
    near(0, K)
    half_first(0, V, 1)
    near(0, V)
    near(0, Q)
    half_then_row(0, K, 0)
    half_first(0, Q, 2)
    half_then_row(0, V, 1)
    row_then_half(1, K, 0)
    row_first(1, V, 1)
    half_then_row(0, Q, 2)
    row_first(1, Q, 2)
    row_then_half(1, V, 1)

    wait(gains, gain_sem)
    table = gains[...].astype(jnp.float32)
    norm_keys(0)
    wait(got.at[0, V], got_sem.at[0, V])
    row_then_half_by_turn(1, Q, 2)
    near(1, K)
    wait(got.at[0, Q], got_sem.at[0, Q])
    near(1, V)
    near(1, Q)
    loop(turns, lambda turn: far_turn(0, turn))
    loop(turns, lambda turn: near_turn(0, turn))
    norm_keys(1)
    wait(got.at[1, V], got_sem.at[1, V])
    loop(turns, lambda turn: send_far(0, turn))
    wait(got.at[1, Q, pl.ds(0, half_rows)], got_sem.at[1, Q])
    loop(turns, lambda turn: near_turn(1, turn))

    def late_turn(turn):
        wait(got.at[1, Q, pl.ds(0, 2 * pair)], late_sem.at[turn])
        far_turn(1, turn)
        send_far(1, turn)

    loop(turns, late_turn)
    loop(turns, lambda turn: relay_turn(0, turn))
    loop(turns, lambda turn: relay_turn(1, turn))

    others = rows * (half_size - 1)
    for sample in range(samples):
        for part in range(3):
            wait(got.at[sample, part, pl.ds(0, others)], near_sent.at[sample, part])
    for slot in range(6):
        wait(by_row.at[0, pl.ds(0, others)], row_sent.at[slot])
        wait(by_row.at[0], half_sent.at[slot])
    wait(done.at[:, 0], out_sent.at[0])
    wait(got.at[0, pl.ds(0, 2), pl.ds(0, others)], out_sent.at[1])
    wait(got.at[0, pl.ds(0, 2), pl.ds(0, others)], relay_sent)
    wait(out, out_sem)

    @pl.when(replica == owner)
    def _():
        loop(replicas - 1, lambda step: wait(gains, gain_sent))


def shards(qkv, master, moment_one, moment_two, grads):
    updated, first_moment, second_moment = adamw(master, moment_one, moment_two, grads)
    layer = updated.astype(jnp.bfloat16)
    groups = lax.axis_size("seq")
    replicas = lax.axis_size("dp")
    _, _, samples, rows, width = qkv.shape
    patches = rows * groups
    attended = pl.pallas_call(
        functools.partial(kernel, groups, replicas),
        out_shape=jax.ShapeDtypeStruct((1, samples, rows, width), jnp.bfloat16),
        in_specs=[pl.BlockSpec(memory_space=pl.ANY), pl.BlockSpec(memory_space=pltpu.VMEM)],
        out_specs=pl.BlockSpec(memory_space=pl.ANY),
        scratch_shapes=[
            pltpu.VMEM((samples, 3, patches, HD), jnp.bfloat16),
            pltpu.VMEM((3, patches // 2, HD), jnp.bfloat16),
            pltpu.VMEM((3, rows, groups // 2 * HD), jnp.bfloat16),
            pltpu.VMEM((samples, patches, HD), jnp.bfloat16),
            pltpu.VMEM((samples, 2, groups // 8, 4 * rows, HD), jnp.bfloat16),
            pltpu.VMEM((samples, groups // 8, 4 * rows, HD), jnp.bfloat16),
            pltpu.VMEM((4, HD), jnp.bfloat16),
            pltpu.SemaphoreType.DMA((samples, 3)),
            pltpu.SemaphoreType.DMA((groups // 8,)),
            pltpu.SemaphoreType.DMA((3,)),
            pltpu.SemaphoreType.DMA((3,)),
            pltpu.SemaphoreType.DMA((samples, groups // 8)),
            pltpu.SemaphoreType.DMA,
            pltpu.SemaphoreType.DMA,
            pltpu.SemaphoreType.DMA((samples, 3)),
            pltpu.SemaphoreType.DMA((6,)),
            pltpu.SemaphoreType.DMA((6,)),
            pltpu.SemaphoreType.DMA((2,)),
            pltpu.SemaphoreType.DMA,
            pltpu.SemaphoreType.DMA,
        ],
        compiler_params=pltpu.CompilerParams(
            collective_id=0, has_side_effects=True, vmem_limit_bytes=48 * 1024 * 1024
        ),
    )(qkv, layer)
    return (attended, updated, first_moment, second_moment)


def solution(mesh):
    placed = (
        P(None, "dp", None, "seq", None),
        P(None, "dp"),
        P(None, "dp"),
        P(None, "dp"),
        P(None, "dp"),
    )
    return jax.shard_map(
        shards,
        mesh=mesh,
        in_specs=placed,
        out_specs=(P("dp", None, "seq", None), P(None, "dp"), P(None, "dp"), P(None, "dp")),
        check_vma=False,
    )
```

time: 135 us -> 125 us (0.926)
  the two profiles are of different devices: /device:TPU:59 before, /device:TPU:71 now
where the time goes in v2:
time: 125 us
  Pallas kernels  120 us (96%)
  local copies, waits for them, and re-layouts  2.86 us (2%)
  other arithmetic  1.36 us (1%)
    pallas_call x1, Pallas kernels, shards(): pl.pallas_call(functools.partial(kernel, groups, replicas), out_shape=jax...  120 us
    unnamed x3, local copies, waits for them, and re-layouts  2.86 us

profile of v2, /device:TPU:71, one launch (start us, length us, event | category | flops | bytes accessed | tf_op | source)
XLA Modules:
  0.0 125.3 jit_solution(17472982682368885149)
XLA Ops:
  0.6 1.4 %fusion.1 = (bf16[4,256]{1,0:T(4,128)(2,1)S(1)}, f32[4,256]{1,0:T(4,128)}, f32[4,256]{1,0:T(4,128)}, f32[4,256]{1,0:T(4,128)}) fusion(f32[4,256]{1,0:T(4,128)} %param.6, f32[4,256]{1,0:T(4,128)} %param.9, f32[4,256]{1,0:T(4,128)} %param.7, f32[4,256]{1,0:T(4,128)} %param.8), kind=kLoop, calls=%fused_computation.4 | loop fusion | flops 16384 | bytes 30720 | tf_op jit(solution)/shard_map/convert_element_type | solution.py:314
  2.0 0.0 copy-start
  2.0 1.9 %copy-done = bf16[3,1,2,64,4096]{4,3,2,1,0:T(8,128)(2,1)S(1)} copy-done((bf16[3,1,2,64,4096]{4,3,2,1,0:T(8,128)(2,1)S(1)}, bf16[3,1,2,64,4096]{4,3,2,1,0:T(8,128)(2,1)}, u32[]{:S(2)}) %copy-start) | copy-done | bytes 3145752
  3.9 120.4 %shard_map.84 = bf16[1,2,64,4096]{3,2,1,0:T(8,128)(2,1)S(1)} custom-call(bf16[3,1,2,64,4096]{4,3,2,1,0:T(8,128)(2,1)S(1)} %copy-done, bf16[4,256]{1,0:T(4,128)(2,1)S(1)} %get-tuple-element.4.layer), custom_call_target="tpu_custom_call" | custom-call | tf_op jit(solution)/shard_map/pallas_call | solution.py:319
  124.3 1.0 copy.10
Async XLA Ops:
  2.0 1.9 %copy-start = (bf16[3,1,2,64,4096]{4,3,2,1,0:T(8,128)(2,1)S(1)}, bf16[3,1,2,64,4096]{4,3,2,1,0:T(8,128)(2,1)}, u32[]{:S(2)}) copy-start(bf16[3,1,2,64,4096]{4,3,2,1,0:T(8,128)(2,1)} %qkv.1) | copy-start | bytes 9437188

commit v3 on v2

--- a/solution.py
+++ b/solution.py
@@ -58,10 +58,10 @@
     lax.fori_loop(0, count, step, 0)
 
 
-def kernel(groups, replicas, qkv, layer, out, got, by_row, by_half, keys, done, relay, gains,
-           got_sem, late_sem, row_sem, half_sem, relay_sem, out_sem, gain_sem,
+def kernel(groups, replicas, stored, layer, out, qkv, got, by_row, by_half, keys, done, relay, gains,
+           load_sem, got_sem, late_sem, row_sem, half_sem, relay_sem, out_sem, gain_sem,
            near_sent, row_sent, half_sent, out_sent, relay_sent, gain_sent):
-    samples, rows = qkv.shape[2], qkv.shape[3]
+    samples, rows = stored.shape[2], stored.shape[3]
     half_size = groups // 2
     chips = half_size // 2
     half_rows = rows * half_size
@@ -106,6 +106,12 @@
     def chip_rows(which, seat):
         return pl.ds(pl.multiple_of(which * half_rows + seat * pair, pair), pair)
 
+    for sample, part in ((0, K), (1, K), (0, V), (0, Q), (1, V), (1, Q)):
+        keep(stored.at[part, 0, sample], qkv.at[part, 0, sample], load_sem.at[sample, part])
+
+    def loaded(sample, part):
+        wait(qkv.at[part, 0, sample], load_sem.at[sample, part])
+
     barrier = pltpu.get_barrier_semaphore()
 
     def greet_row(step, carry):
@@ -118,12 +124,132 @@
         pl.semaphore_signal(barrier, 1, device_id=(other, me), device_id_type=MESH)
         return carry
 
+    pl.semaphore_signal(barrier, 1, device_id=(replica, opposite), device_id_type=MESH)
     lax.fori_loop(0, half_size - 1, greet_row, 0)
-    pl.semaphore_signal(barrier, 1, device_id=(replica, opposite), device_id_type=MESH)
     lax.fori_loop(1, replicas, greet_dp, 0)
     pl.semaphore_wait(barrier, half_size - 1 + 1 + replicas - 1)
 
     own_layer = layer.at[:, pl.ds(pl.multiple_of(me * HD % layer.shape[1], HD), HD)]
+
+    def near(sample, part):
+        target = got.at[sample, part, at_rows(me), :]
+        arrived = got_sem.at[sample, part]
+
+        def send(step, carry):
+            device = half * half_size + peer(step)
+            source = qkv.at[part, 0, sample, :, columns(device)]
+            push(source, target, near_sent.at[sample, part], arrived, device)
+            return carry
+
+        lax.fori_loop(0, half_size - 1, send, 0)
+        keep(qkv.at[part, 0, sample, :, columns(me)], target, arrived)
+
+    def row_first(sample, part, slot):
+        target = by_row.at[slot, at_rows(place), :]
+
+        def send(step, carry):
+            seat = peer(step)
+            source = qkv.at[part, 0, sample, :, columns((1 - half) * half_size + seat)]
+            push(source, target, row_sent.at[slot], row_sem.at[slot], half * half_size + seat)
+            return carry
+
+        lax.fori_loop(0, half_size - 1, send, 0)
+        source = qkv.at[part, 0, sample, :, columns(opposite)]
+        keep(source, target, row_sem.at[slot])
+
+    def row_then_half(sample, part, slot):
+        wait(by_row.at[slot], row_sem.at[slot])
+        at = pl.ds(pl.multiple_of(half * half_rows, half_rows), half_rows)
+        push(
+            by_row.at[slot], got.at[sample, part, at, :], half_sent.at[slot],
+            got_sem.at[sample, part], opposite,
+        )
+
+    def row_then_half_by_turn(sample, part, slot):
+        wait(by_row.at[slot], row_sem.at[slot])
+
+        def send(turn):
+            for seat in spots(turn):
+                source = by_row.at[slot, pl.ds(pl.multiple_of(seat * pair, pair), pair), :]
+                target = got.at[sample, part, chip_rows(half, seat), :]
+                push(source, target, half_sent.at[slot], late_sem.at[turn], opposite)
+
+        loop(turns, send)
+
+    def half_first(sample, part, slot):
+        source = qkv.at[part, 0, sample, :, columns((1 - half) * half_size, half_size)]
+        push(source, by_half.at[slot], half_sent.at[3 + slot], half_sem.at[slot], opposite)
+
+    def half_then_row(sample, part, slot):
+        target = got.at[sample, part, at_rows(opposite), :]
+        arrived = got_sem.at[sample, part]
+
+        def send(step, carry):
+            seat = peer(step)
+            source = by_half.at[slot, :, columns(seat)]
+            push(source, target, row_sent.at[3 + slot], arrived, half * half_size + seat)
+            return carry
+
+        lax.fori_loop(0, half_size - 1, send, 0)
+        keep(by_half.at[slot, :, columns(place)], target, arrived)
+
+    def norm_keys(sample):
+        wait(got.at[sample, K], got_sem.at[sample, K])
+
+        def norm_rows(step):
+            at = pl.ds(pl.multiple_of(step * BLOCK, BLOCK), BLOCK)
+            keys[sample, at, :] = normalize(got[sample, K, at, :], table[2:3], table[3:4])
+
+        loop(keys.shape[1] // BLOCK, norm_rows)
+
+    def attend_turn(sample, turn, which):
+        ats = [chip_rows(which, seat) for seat in spots(turn)]
+        block = jnp.concatenate([got[sample, Q, at, :] for at in ats], axis=0)
+        queries = normalize(block, table[0:1], table[1:2])
+        return attend(queries, keys[sample], got[sample, V])
+
+    def far_turn(sample, turn):
+        done[sample, 0, turn] = attend_turn(sample, turn, 1 - half)
+
+    def send_far(sample, turn):
+        push(
+            done.at[sample, 0, turn], relay.at[sample, turn], out_sent.at[0],
+            relay_sem.at[sample, turn], opposite,
+        )
+
+    def hand_out(source, head, sample, turn, sent):
+        target = out.at[0, sample, :, columns(head)]
+        for side, seat in enumerate(spots(turn)):
+            for unit in range(2):
+                piece = source.at[pl.ds(side * pair + unit * rows, rows), :]
+                device = half * half_size + seat * 2 + unit
+
+                @pl.when(device != me)
+                def _():
+                    push(piece, target, sent, out_sem, device)
+
+                @pl.when(device == me)
+                def _():
+                    keep(piece, target, out_sem)
+
+    def near_turn(sample, turn):
+        done[sample, 1, turn] = attend_turn(sample, turn, half)
+        hand_out(done.at[sample, 1, turn], me, sample, turn, out_sent.at[1])
+
+    def relay_turn(sample, turn):
+        wait(relay.at[sample, turn], relay_sem.at[sample, turn])
+        hand_out(relay.at[sample, turn], opposite, sample, turn, relay_sent)
+
+    loaded(0, K)
+    half_first(0, K, 0)
+    loaded(1, K)
+    row_first(1, K, 0)
+    loaded(0, V)
+    half_first(0, V, 1)
+    near(0, K)
+    near(0, V)
+    loaded(0, Q)
+    near(0, Q)
 
     @pl.when(replica == owner)
     def _():
@@ -141,130 +267,19 @@
         lax.fori_loop(1, replicas, give, 0)
         keep(own_layer, gains, gain_sem)
 
-    def near(sample, part):
-        target = got.at[sample, part, at_rows(me), :]
-        arrived = got_sem.at[sample, part]
-
-        def send(step, carry):
-            device = half * half_size + peer(step)
-            source = qkv.at[part, 0, sample, :, columns(device)]
-            push(source, target, near_sent.at[sample, part], arrived, device)
-            return carry
-
-        lax.fori_loop(0, half_size - 1, send, 0)
-        keep(qkv.at[part, 0, sample, :, columns(me)], target, arrived)
-
-    def row_first(sample, part, slot):
-        target = by_row.at[slot, at_rows(place), :]
-
-        def send(step, carry):
-            seat = peer(step)
-            source = qkv.at[part, 0, sample, :, columns((1 - half) * half_size + seat)]
-            push(source, target, row_sent.at[slot], row_sem.at[slot], half * half_size + seat)
-            return carry
-
-        lax.fori_loop(0, half_size - 1, send, 0)
-        source = qkv.at[part, 0, sample, :, columns(opposite)]
-        keep(source, target, row_sem.at[slot])
-
-    def row_then_half(sample, part, slot):
-        wait(by_row.at[slot], row_sem.at[slot])
-        at = pl.ds(pl.multiple_of(half * half_rows, half_rows), half_rows)
-        push(
-            by_row.at[slot], got.at[sample, part, at, :], half_sent.at[slot],
-            got_sem.at[sample, part], opposite,
-        )
-
-    def row_then_half_by_turn(sample, part, slot):
-        wait(by_row.at[slot], row_sem.at[slot])
-
-        def send(turn):
-            for seat in spots(turn):
-                source = by_row.at[slot, pl.ds(pl.multiple_of(seat * pair, pair), pair), :]
-                target = got.at[sample, part, chip_rows(half, seat), :]
-                push(source, target, half_sent.at[slot], late_sem.at[turn], opposite)
-
-        loop(turns, send)
-
-    def half_first(sample, part, slot):
-        source = qkv.at[part, 0, sample, :, columns((1 - half) * half_size, half_size)]
-        push(source, by_half.at[slot], half_sent.at[3 + slot], half_sem.at[slot], opposite)
-
-    def half_then_row(sample, part, slot):
-        wait(by_half.at[slot], half_sem.at[slot])
-        target = got.at[sample, part, at_rows(opposite), :]
-        arrived = got_sem.at[sample, part]
-
-        def send(step, carry):
-            seat = peer(step)
-            source = by_half.at[slot, :, columns(seat)]
-            push(source, target, row_sent.at[3 + slot], arrived, half * half_size + seat)
-            return carry
-
-        lax.fori_loop(0, half_size - 1, send, 0)
-        keep(by_half.at[slot, :, columns(place)], target, arrived)
-
-    def norm_keys(sample):
-        wait(got.at[sample, K], got_sem.at[sample, K])
-
-        def norm_rows(step):
-            at = pl.ds(pl.multiple_of(step * BLOCK, BLOCK), BLOCK)
-            keys[sample, at, :] = normalize(got[sample, K, at, :], table[2:3], table[3:4])
-
-        loop(keys.shape[1] // BLOCK, norm_rows)
-
-    def attend_turn(sample, turn, which):
-        ats = [chip_rows(which, seat) for seat in spots(turn)]
-        block = jnp.concatenate([got[sample, Q, at, :] for at in ats], axis=0)
-        queries = normalize(block, table[0:1], table[1:2])
-        return attend(queries, keys[sample], got[sample, V])
-
-    def far_turn(sample, turn):
-        done[sample, 0, turn] = attend_turn(sample, turn, 1 - half)
-
-    def send_far(sample, turn):
-        push(
-            done.at[sample, 0, turn], relay.at[sample, turn], out_sent.at[0],
-            relay_sem.at[sample, turn], opposite,
-        )
-
-    def hand_out(source, head, sample, turn, sent):
-        target = out.at[0, sample, :, columns(head)]
-        for side, seat in enumerate(spots(turn)):
-            for unit in range(2):
-                piece = source.at[pl.ds(side * pair + unit * rows, rows), :]
-                device = half * half_size + seat * 2 + unit
-
-                @pl.when(device != me)
-                def _():
-                    push(piece, target, sent, out_sem, device)
-
-                @pl.when(device == me)
-                def _():
-                    keep(piece, target, out_sem)
-
-    def near_turn(sample, turn):
-        done[sample, 1, turn] = attend_turn(sample, turn, half)
-        hand_out(done.at[sample, 1, turn], me, sample, turn, out_sent.at[1])
-
-    def relay_turn(sample, turn):
-        wait(relay.at[sample, turn], relay_sem.at[sample, turn])
-        hand_out(relay.at[sample, turn], opposite, sample, turn, relay_sent)
-
-    half_first(0, K, 0)
-    row_first(1, K, 0)
-    near(0, K)
-    half_first(0, V, 1)
-    near(0, V)
-    near(0, Q)
+    wait(by_half.at[0], half_sem.at[0])
+    half_first(0, Q, 2)
     half_then_row(0, K, 0)
-    half_first(0, Q, 2)
+    wait(by_half.at[1], half_sem.at[1])
+    row_then_half(1, K, 0)
     half_then_row(0, V, 1)
-    row_then_half(1, K, 0)
+    loaded(1, V)
     row_first(1, V, 1)
+    wait(by_half.at[2], half_sem.at[2])
+    row_then_half(1, V, 1)
     half_then_row(0, Q, 2)
+    loaded(1, Q)
     row_first(1, Q, 2)
-    row_then_half(1, V, 1)
 
     wait(gains, gain_sem)
     table = gains[...].astype(jnp.float32)
@@ -319,9 +334,10 @@
     attended = pl.pallas_call(
         functools.partial(kernel, groups, replicas),
         out_shape=jax.ShapeDtypeStruct((1, samples, rows, width), jnp.bfloat16),
-        in_specs=[pl.BlockSpec(memory_space=pl.ANY), pl.BlockSpec(memory_space=pltpu.VMEM)],
+        in_specs=[pl.BlockSpec(memory_space=pltpu.HBM), pl.BlockSpec(memory_space=pltpu.VMEM)],
         out_specs=pl.BlockSpec(memory_space=pl.ANY),
         scratch_shapes=[
+            pltpu.VMEM(qkv.shape, jnp.bfloat16),
             pltpu.VMEM((samples, 3, patches, HD), jnp.bfloat16),
             pltpu.VMEM((3, patches // 2, HD), jnp.bfloat16),
             pltpu.VMEM((3, rows, groups // 2 * HD), jnp.bfloat16),
@@ -329,6 +345,7 @@
             pltpu.VMEM((samples, 2, groups // 8, 4 * rows, HD), jnp.bfloat16),
             pltpu.VMEM((samples, groups // 8, 4 * rows, HD), jnp.bfloat16),
             pltpu.VMEM((4, HD), jnp.bfloat16),
+            pltpu.SemaphoreType.DMA((samples, 3)),
             pltpu.SemaphoreType.DMA((samples, 3)),
             pltpu.SemaphoreType.DMA((groups // 8,)),
             pltpu.SemaphoreType.DMA((3,)),
@@ -344,7 +361,7 @@
             pltpu.SemaphoreType.DMA,
         ],
         compiler_params=pltpu.CompilerParams(
-            collective_id=0, has_side_effects=True, vmem_limit_bytes=48 * 1024 * 1024
+            collective_id=0, has_side_effects=True, vmem_limit_bytes=60 * 1024 * 1024
         ),
     )(qkv, layer)
     return (attended, updated, first_moment, second_moment)

time: 125 us -> 125 us (level)
  the two profiles are of different devices: /device:TPU:71 before, /device:TPU:135 now
where the time goes in v3:
time: 125 us
  Pallas kernels  121 us (97%)
  local copies, waits for them, and re-layouts  2.29 us (2%)
  other arithmetic  1.36 us (1%)
    pallas_call x1, Pallas kernels, shards(): pl.pallas_call(functools.partial(kernel, groups, replicas), out_shape=jax...  121 us

profile of v3, /device:TPU:135, one launch (start us, length us, event | category | flops | bytes accessed | tf_op | source)
XLA Modules:
  0.0 125.3 jit_solution(6841556083052619666)
XLA Ops:
  0.6 1.4 %fusion.1 = (bf16[4,256]{1,0:T(4,128)(2,1)}, f32[4,256]{1,0:T(4,128)}, f32[4,256]{1,0:T(4,128)}, f32[4,256]{1,0:T(4,128)}) fusion(f32[4,256]{1,0:T(4,128)} %param.6, f32[4,256]{1,0:T(4,128)} %param.9, f32[4,256]{1,0:T(4,128)} %param.7, f32[4,256]{1,0:T(4,128)} %param.8), kind=kLoop, calls=%fused_computation.4 | loop fusion | flops 16384 | bytes 30720 | tf_op jit(solution)/shard_map/convert_element_type | solution.py:329
  2.0 121.0 %shard_map.84 = bf16[1,2,64,4096]{3,2,1,0:T(8,128)(2,1)} custom-call(bf16[3,1,2,64,4096]{4,3,2,1,0:T(8,128)(2,1)} %stored.1, bf16[4,256]{1,0:T(4,128)(2,1)} %get-tuple-element.4.layer), custom_call_target="tpu_custom_call" | custom-call | tf_op jit(solution)/shard_map/pallas_call | solution.py:334
  123.0 2.3 %copy.10 = bf16[1,2,64,4096]{3,2,1,0:T(8,128)(2,1)} copy(bf16[1,2,64,4096]{3,2,1,0:T(8,128)(2,1)} %shard_map.84) | data formatting | bytes 2097152

commit v4 on v3

--- a/solution.py
+++ b/solution.py
@@ -361,9 +361,9 @@
             pltpu.SemaphoreType.DMA,
         ],
         compiler_params=pltpu.CompilerParams(
-            collective_id=0, has_side_effects=True, vmem_limit_bytes=60 * 1024 * 1024
+            collective_id=0, has_side_effects=True, vmem_limit_bytes=48 * 1024 * 1024
         ),
-    )(qkv, layer)
+    )(pltpu.with_memory_space_constraint(qkv, pltpu.HBM), layer)
     return (attended, updated, first_moment, second_moment)
 
 

time: 125 us -> 125 us (level)
  the two profiles are of different devices: /device:TPU:135 before, /device:TPU:131 now
where the time goes in v4:
time: 125 us
  Pallas kernels  122 us (98%)
  other arithmetic  1.36 us (1%)
    pallas_call x1, Pallas kernels, shards(): pl.pallas_call(functools.partial(kernel, groups, replicas), out_shape=jax...  122 us

profile of v4, /device:TPU:131, one launch (start us, length us, event | category | flops | bytes accessed | tf_op | source)
XLA Modules:
  0.0 124.6 jit_solution(16710488984081557650)
XLA Ops:
  0.6 1.4 %fusion.1 = (bf16[4,256]{1,0:T(4,128)(2,1)S(1)}, f32[4,256]{1,0:T(4,128)}, f32[4,256]{1,0:T(4,128)}, f32[4,256]{1,0:T(4,128)}) fusion(f32[4,256]{1,0:T(4,128)} %param.6, f32[4,256]{1,0:T(4,128)} %param.9, f32[4,256]{1,0:T(4,128)} %param.7, f32[4,256]{1,0:T(4,128)} %param.8), kind=kLoop, calls=%fused_computation.4 | loop fusion | flops 16384 | bytes 30720 | tf_op jit(solution)/shard_map/convert_element_type | solution.py:329
  2.0 121.6 %shard_map.84 = bf16[1,2,64,4096]{3,2,1,0:T(8,128)(2,1)S(1)} custom-call(bf16[3,1,2,64,4096]{4,3,2,1,0:T(8,128)(2,1)} %stored.1, bf16[4,256]{1,0:T(4,128)(2,1)S(1)} %get-tuple-element.4.layer), custom_call_target="tpu_custom_call" | custom-call | tf_op jit(solution)/shard_map/pallas_call | solution.py:334
  123.6 1.0 copy.10

commit v5 on v4

--- a/solution.py
+++ b/solution.py
@@ -293,8 +293,8 @@
     loop(turns, lambda turn: far_turn(0, turn))
     loop(turns, lambda turn: near_turn(0, turn))
     norm_keys(1)
+    loop(turns, lambda turn: send_far(0, turn))
     wait(got.at[1, V], got_sem.at[1, V])
-    loop(turns, lambda turn: send_far(0, turn))
     wait(got.at[1, Q, pl.ds(0, half_rows)], got_sem.at[1, Q])
     loop(turns, lambda turn: near_turn(1, turn))
 

time: 125 us -> 125 us (level)
  no operation moved by 1% of the time
where the time goes in v5:
time: 125 us
  Pallas kernels  122 us (98%)
  other arithmetic  1.36 us (1%)
    pallas_call x1, Pallas kernels, shards(): pl.pallas_call(functools.partial(kernel, groups, replicas), out_shape=jax...  122 us

profile of v5, /device:TPU:131, one launch (start us, length us, event | category | flops | bytes accessed | tf_op | source)
XLA Modules:
  0.0 124.6 jit_solution(5647015192793345671)
XLA Ops:
  0.6 1.4 %fusion.1 = (bf16[4,256]{1,0:T(4,128)(2,1)S(1)}, f32[4,256]{1,0:T(4,128)}, f32[4,256]{1,0:T(4,128)}, f32[4,256]{1,0:T(4,128)}) fusion(f32[4,256]{1,0:T(4,128)} %param.6, f32[4,256]{1,0:T(4,128)} %param.9, f32[4,256]{1,0:T(4,128)} %param.7, f32[4,256]{1,0:T(4,128)} %param.8), kind=kLoop, calls=%fused_computation.4 | loop fusion | flops 16384 | bytes 30720 | tf_op jit(solution)/shard_map/convert_element_type | solution.py:329
  2.0 121.6 %shard_map.84 = bf16[1,2,64,4096]{3,2,1,0:T(8,128)(2,1)S(1)} custom-call(bf16[3,1,2,64,4096]{4,3,2,1,0:T(8,128)(2,1)} %stored.1, bf16[4,256]{1,0:T(4,128)(2,1)S(1)} %get-tuple-element.4.layer), custom_call_target="tpu_custom_call" | custom-call | tf_op jit(solution)/shard_map/pallas_call | solution.py:334
  123.6 1.0 copy.10
